TPU v7x, 256 devices: a whole 4x4x8 slice. The times are simulated.
256 devices in a mesh: row: 16 (over y, x_hi, core), col: 16 (over z, x_lo).
Axes of the slice: x: 4 (x_hi: 2, x_lo: 2; x = x_hi * 2 + x_lo), y: 4, z: 8, core: 2. Of those that a mesh axis runs over, the one named last changes fastest.
Arguments:
- cell_batch: bfloat16 [2048, 20480], P('col', 'row'), may hold values from -6 to 6
- cov_prior: bfloat16 [20480, 20480], P('row', 'col'), as said below
- omega_prior: bfloat16 [20480, 20480], P('row', 'col'), as said below
Outputs:
- cov_updated: bfloat16 [20480, 20480], P('row', 'col')
- omega_panel: bfloat16 [1024, 20480], P('col', 'row')
- column_objective: float32 [1024], P('col')
Inputs may be any that keep to these rules, and one draw needn't show every extreme that they name: `cov_prior`: Symmetric; its diagonal entries lie between 0.5 and 1.5. `omega_prior`: Symmetric; its diagonal entries lie between 1 and 4.
All inputs are finite; a program needn't handle non-finite values.
Results may differ from a plain program's by a relative error of at most 0.0047.
Values may be sent and summed in bfloat16 or wider, within the bound.
A program may use at most 128 MiB of HBM per device.

v0:
```python
import jax
import jax.numpy as jnp
from jax import lax
from jax.sharding import PartitionSpec as P

P_SIZE = 20480
PW = 64
decay_weight = 0.5
step_size = 0.2
penalty = 1.0


def broadcast(value, axis, source):
    kept = jnp.where(lax.axis_index(axis) == source, value, 0).astype(value.dtype)
    return lax.psum(kept, axis)


def contract(left_rows, right_rows):
    return lax.dot_general(
        left_rows, right_rows, (((1,), (1,)), ((), ())), preferred_element_type=jnp.float32
    )


def per_device(cell_batch, cov_prior, omega_prior):
    rows_count = lax.axis_size("row")
    cols_count = lax.axis_size("col")
    fold_ratio = rows_count // cols_count
    row_width = omega_prior.shape[0]
    col_number = lax.axis_index("col")
    row_number = lax.axis_index("row")
    own_slab = lax.all_gather(cell_batch, "col", axis=0, tiled=True)
    mirrored = broadcast(own_slab, "row", col_number * fold_ratio + 0)
    product = lax.dot_general(
        own_slab, mirrored, (((0,), (0,)), ((), ())), preferred_element_type=jnp.float32
    )
    scale_new = (1.0 - decay_weight) / own_slab.shape[0]
    cov_updated = (decay_weight * cov_prior.astype(jnp.float32) + scale_new * product).astype(
        jnp.bfloat16
    )
    cov_rows, omega_rows = (
        lax.all_gather(cov_updated[:PW], "row", axis=0, tiled=True),
        lax.all_gather(omega_prior[:PW], "row", axis=0, tiled=True),
    )
    own_rows = PW * fold_ratio
    omega_cols_half = (
        omega_prior.reshape(row_width, fold_ratio, row_width)[:, :, :PW]
        .reshape(row_width, own_rows)
        .T
    )
    omega_vals = omega_cols_half.astype(jnp.float32)
    positions = lax.iota(jnp.int32, own_rows)
    same_block = row_number == col_number * fold_ratio + positions // PW
    diagonal = same_block[:, None] & (
        (positions % PW)[:, None] == lax.iota(jnp.int32, row_width)[None, :]
    )
    own_diag = jnp.where(diagonal, omega_vals, jnp.float32(1.0))
    inverse = jnp.where(diagonal, 1.0 / own_diag, jnp.float32(0.0))
    logs = jnp.sum(jnp.where(diagonal, jnp.log(own_diag), jnp.float32(0.0)), axis=1)
    lasso = penalty * jnp.sum(jnp.where(diagonal, jnp.float32(0.0), jnp.abs(omega_vals)), axis=1)
    summed = lax.psum_scatter(
        jnp.concatenate(
            [contract(cov_rows, omega_prior), contract(omega_rows, cov_updated)], axis=1
        ),
        "col",
        scatter_dimension=0,
        tiled=True,
    )
    first_sum = summed[:, :row_width]
    second_sum = summed[:, row_width:]
    both_sum = first_sum + second_sum
    quadratic = 0.5 * jnp.sum(omega_vals * second_sum, axis=1)
    column_objective = lax.psum(quadratic + lasso - logs, "row") / P_SIZE
    gradient = 0.5 * both_sum - inverse
    stepped = omega_vals - step_size * gradient
    shrunk = jnp.sign(stepped) * jnp.maximum(jnp.abs(stepped) - step_size * penalty, 0.0)
    omega_panel = jnp.where(diagonal, stepped, shrunk).astype(jnp.bfloat16)
    return (cov_updated, omega_panel, column_objective)


def solution(mesh):
    return jax.shard_map(
        per_device,
        mesh=mesh,
        in_specs=(P("col", "row"), P("row", "col"), P("row", "col")),
        out_specs=(P("row", "col"), P("col", "row"), P("col")),
        check_vma=False,
    )
```

profile of v0, /device:TPU:32, one launch (start us, length us, event | category | flops | bytes accessed | tf_op | source)
XLA Modules:
  0.0 705.4 jit_solution(16349236336308614956)
XLA Ops:
  7.2 0.0 all-gather.4.cloned.1.call-start
  7.2 0.7 all-gather.4.cloned.1.call-update
  7.9 0.0 all-reduce.2.cloned.1.call-start
  8.0 123.7 %all-gather.4.cloned.1.call-done = bf16[2048,1280]{1,0:T(8,128)(2,1)} async-done(((bf16[128,1280]{1,0:T(8,128)(2,1)}), bf16[2048,1280]{1,0:T(8,128)(2,1)}) %all-gather.4.cloned.1.call-update) | async-done | bytes 5242896 | tf_op jit(solution)/shard_map/all_gather | solution.py:31
  131.6 2.7 broadcast_select_fusion
  134.3 0.0 all-gather.8.cloned.1.call-start
  134.4 1.9 copy-done
  136.2 0.7 slice.17
  136.9 0.0 all-gather.6.cloned.1.call-start
  137.0 167.5 %all-reduce.2.cloned.1.call-done = bf16[2048,1280]{1,0:T(8,128)(2,1)} async-done(((bf16[2048,1280]{1,0:T(8,128)(2,1)}), bf16[2048,1280]{1,0:T(8,128)(2,1)}) %all-reduce.2.cloned.1.call-update) | async-done | bytes 5242896 | tf_op jit(solution)/shard_map/psum | solution.py:15
  304.5 11.3 %fusion.2 = bf16[1280,1280]{1,0:T(8,128)(2,1)S(1)} fusion(bf16[2048,1280]{1,0:T(8,128)(2,1)} %all-reduce.2.cloned.1.call-done, bf16[2048,1280]{1,0:T(8,128)(2,1)} %all-gather.4.cloned.1.call-done, bf16[1280,1280]{1,0:T(8,128)(2,1)} %param.4), kind=kOutput, calls=%fused_computation.4 | convolution fusion | flops 6719078400 | bytes 17039360 | tf_op jit(solution)/shard_map/dot_general | solution.py:33
  315.8 1.7 copy-done.1
  317.5 0.7 slice.21
  318.2 0.0 reduce-scatter.2.cloned.1.call-start
  318.2 43.7 %all-gather.8.cloned.1.call-done = bf16[1024,1280]{1,0:T(8,128)(2,1)} async-done(((bf16[64,1280]{1,0:T(8,128)(2,1)}), bf16[1024,1280]{1,0:T(8,128)(2,1)}) %all-gather.8.cloned.1.call-update) | async-done | bytes 2621456 | tf_op jit(solution)/shard_map/all_gather | solution.py:42
  362.0 8.7 %convolution_bitcast_fusion = f32[1024,1280]{1,0:T(8,128)} fusion(bf16[1280,1280]{1,0:T(8,128)(2,1)} %copy-done.1, bf16[1024,1280]{1,0:T(8,128)(2,1)} %all-gather.8.cloned.1.call-done), kind=kOutput, calls=%fused_computation.6 | convolution fusion | flops 3355443200 | bytes 11141120 | tf_op jit(solution)/shard_map/dot_general | solution.py:19
  370.6 47.0 %all-gather.6.cloned.1.call-done = bf16[1024,1280]{1,0:T(8,128)(2,1)} async-done(((bf16[64,1280]{1,0:T(8,128)(2,1)}), bf16[1024,1280]{1,0:T(8,128)(2,1)}) %all-gather.6.cloned.1.call-update) | async-done | bytes 2621456 | tf_op jit(solution)/shard_map/all_gather | solution.py:41
  417.7 7.6 %fusion.21 = f32[1024,1280]{1,0:T(8,128)} fusion(bf16[1024,1280]{1,0:T(8,128)(2,1)} %all-gather.6.cloned.1.call-done, bf16[1280,1280]{1,0:T(8,128)(2,1)S(1)} %copy-done), kind=kOutput, calls=%fused_computation.37 | convolution fusion | flops 3355443200 | bytes 11141120 | tf_op jit(solution)/shard_map/dot_general | solution.py:19
  425.2 9.2 %pad_maximum_fusion = f32[1024,2560]{1,0:T(8,128)} fusion(f32[1024,1280]{1,0:T(8,128)} %convolution_bitcast_fusion, f32[1024,1280]{1,0:T(8,128)} %fusion.21), kind=kLoop, calls=%fused_computation | loop fusion | flops 2621440 | bytes 20971520 | tf_op jit(solution)/shard_map/concatenate | solution.py:61
  434.5 4.0 copy.6
  438.5 219.7 %reduce-scatter.2.cloned.1.call-done = f32[64,2560]{1,0:T(8,128)} async-done(((f32[1024,2560]{1,0:T(8,128)}), f32[64,2560]{1,0:T(8,128)}) %reduce-scatter.2.cloned.1.call-update) | async-done | bytes 655376 | tf_op jit(solution)/shard_map/reduce_scatter | solution.py:60
  658.3 2.3 fusion.17
  660.6 37.7 %psum.15 = f32[64]{0:T(128)S(1)} all-reduce(f32[64]{0:T(128)S(1)} %add_subtract_fusion), channel_id=1, replica_groups=mesh['row'=16,'col'=16] {'row'}, use_global_device_ids=true, to_apply=%region_5.6 | all-reduce | flops 64 | bytes 512 | tf_op jit(solution)/shard_map/psum | solution.py:72
  698.3 0.5 broadcast_multiply_fusion
  (9 shorter events, 0.1 us)
Async XLA Ops:
  7.2 124.4 %all-gather.4.cloned.1.call-start = ((), (), s32[]{:S(2)}) async-start(), calls=%async_computation.1 | async-start | bytes 5570560 | tf_op jit(solution)/shard_map/all_gather | solution.py:31
  7.9 296.6 %all-reduce.2.cloned.1.call-start = ((), (), s32[]{:S(2)}) async-start(), calls=%async_computation.2 | async-start | bytes 10485760 | tf_op jit(solution)/shard_map/psum | solution.py:15
  134.3 1.9 copy-start
  134.3 227.6 %all-gather.8.cloned.1.call-start = ((), (), s32[]{:S(2)}) async-start(), calls=%async_computation.4 | async-start | bytes 2785280 | tf_op jit(solution)/shard_map/all_gather | solution.py:42
  136.9 280.7 %all-gather.6.cloned.1.call-start = ((), (), s32[]{:S(2)}) async-start(), calls=%async_computation.3 | async-start | bytes 2785280 | tf_op jit(solution)/shard_map/all_gather | solution.py:41
  315.8 1.7 copy-start.1
  318.2 340.1 %reduce-scatter.2.cloned.1.call-start = ((), (), s32[]{:S(2)}) async-start(), calls=%async_computation.5 | async-start | bytes 11141120 | tf_op jit(solution)/shard_map/reduce_scatter | solution.py:60
Sparse Core Ops, SparseCore 0:
  9.8 121.7 all-gather.3
  134.5 169.9 all-reduce.1
  307.8 54.0 all-gather.7
  364.6 53.0 all-gather.5
  434.6 223.6 reduce-scatter.1
where the time goes:
time: 706 us; the launch traced here: 705 us
  waiting for transfers between devices  602 us (85%)
  blocking collectives  37.7 us (5%)
  matrix products  27.5 us (4%)
  other arithmetic  14.8 us (2%)
  between operations  13.8 us (2%)
  local copies, waits for them, and re-layouts  8.93 us (1%)
    reduce_scatter x1, waiting for transfers between devices, per_device(): lax.psum_scatter(jnp.concatenate([contract(cov_rows, omega_prior), contra...  220 us
    psum x1, waiting for transfers between devices, broadcast(): return lax.psum(kept, axis)  167 us
    all_gather x1, waiting for transfers between devices, per_device(): own_slab = lax.all_gather(cell_batch, 'col', axis=0, tiled=True)  124 us
    all_gather x1, waiting for transfers between devices, per_device(): lax.all_gather(cov_updated[:PW], 'row', axis=0, tiled=True)  47 us
    all_gather x1, waiting for transfers between devices, per_device(): lax.all_gather(omega_prior[:PW], 'row', axis=0, tiled=True)  43.7 us
    psum x1, blocking collectives, per_device(): column_objective = lax.psum(quadratic + lasso - logs, 'row') / P_SIZE  37.7 us
    dot_general x2, matrix products, contract(): lax.dot_general(left_rows, right_rows, (((1,), (1,)), ((), ())), preferre...  16.2 us
  transfers between devices with their start and end apart: 5, of which 5 were waited for; matrix products, arithmetic and copies ran while one was open for 4% of the time, Pallas kernels for 0%

commit v1 on v0

--- a/solution.py
+++ b/solution.py
@@ -28,7 +28,9 @@
     row_width = omega_prior.shape[0]
     col_number = lax.axis_index("col")
     row_number = lax.axis_index("row")
-    own_slab = lax.all_gather(cell_batch, "col", axis=0, tiled=True)
+    own_slab = jnp.concatenate(
+        lax.all_to_all(jnp.stack([cell_batch] * lax.axis_size("col")), "col", 0, 0), axis=0
+    )
     mirrored = broadcast(own_slab, "row", col_number * fold_ratio + 0)
     product = lax.dot_general(
         own_slab, mirrored, (((0,), (0,)), ((), ())), preferred_element_type=jnp.float32

time: 706 us -> 715 us (1.013)
  starting transfers between devices: 0.2 us -> 9.68 us
    all_gather x1 -> x0, waiting for transfers between devices: 124 us -> none  [per_device(): own_slab = lax.all_gather(cell_batch, 'col', axis=0, tiled=True)]
    all_to_all x0 -> x1, waiting for transfers between devices: none -> 119 us  [per_device(): lax.all_to_all(jnp.stack([cell_batch] * lax.axis_size('col')), 'col', 0, 0)]
    all_to_all x0 -> x1, starting transfers between devices: none -> 9.51 us  [per_device(): lax.all_to_all(jnp.stack([cell_batch] * lax.axis_size('col')), 'col', 0, 0)]
where the time goes in v1:
time: 715 us
  waiting for transfers between devices  596 us (83%)
  blocking collectives  37.7 us (5%)
  matrix products  27.5 us (4%)
  other arithmetic  17.3 us (2%)
  between operations  13.8 us (2%)
  local copies, waits for them, and re-layouts  12.7 us (2%)
  starting transfers between devices  9.68 us (1%)
    reduce_scatter x1, waiting for transfers between devices, per_device(): lax.psum_scatter(jnp.concatenate([contract(cov_rows, omega_prior), contra...  220 us
    psum x1, waiting for transfers between devices, broadcast(): return lax.psum(kept, axis)  167 us
    all_to_all x1, waiting for transfers between devices, per_device(): lax.all_to_all(jnp.stack([cell_batch] * lax.axis_size('col')), 'col', 0, 0)  119 us
    all_gather x1, waiting for transfers between devices, per_device(): lax.all_gather(cov_updated[:PW], 'row', axis=0, tiled=True)  47.2 us
    all_gather x1, waiting for transfers between devices, per_device(): lax.all_gather(omega_prior[:PW], 'row', axis=0, tiled=True)  43.7 us
    psum x1, blocking collectives, per_device(): column_objective = lax.psum(quadratic + lasso - logs, 'row') / P_SIZE  37.7 us
    dot_general x2, matrix products, contract(): lax.dot_general(left_rows, right_rows, (((1,), (1,)), ((), ())), preferre...  16.2 us
  transfers between devices with their start and end apart: 5, of which 5 were waited for; matrix products, arithmetic and copies ran while one was open for 4% of the time, Pallas kernels for 0%

profile of v1, /device:TPU:32, one launch (start us, length us, event | category | flops | bytes accessed | tf_op | source)
XLA Modules:
  0.0 714.8 jit_solution(11586458155309151134)
XLA Ops:
  7.2 3.8 stack.2
  11.0 9.5 %all-to-all-start = ((bf16[16,128,1280]{2,1,0:T(8,128)(2,1)}), bf16[16,128,1280]{2,1,0:T(8,128)(2,1)}, u32[]{:S(2)}, u32[]{:S(2)}) async-start(bf16[16,128,1280]{2,1,0:T(8,128)(2,1)} %stack.2), calls=%async_computation | async-start | bytes 10485760 | tf_op jit(solution)/shard_map/all_to_all | solution.py:32
  20.5 0.0 all-reduce.2.cloned.1.call-start
  20.6 118.8 %all-to-all-done = bf16[16,128,1280]{2,1,0:T(8,128)(2,1)} async-done(((bf16[16,128,1280]{2,1,0:T(8,128)(2,1)}), bf16[16,128,1280]{2,1,0:T(8,128)(2,1)}, u32[]{:S(2)}, u32[]{:S(2)}) %all-to-all-start) | async-done | bytes 5242912 | tf_op jit(solution)/shard_map/all_to_all | solution.py:32
  139.4 5.2 broadcast_select_fusion
  144.6 0.0 all-gather.5.cloned.1.call-start
  144.6 1.9 copy-done
  146.5 0.7 slice.17
  147.2 0.0 all-gather.3.cloned.1.call-start
  147.2 166.6 %all-reduce.2.cloned.1.call-done = bf16[2048,1280]{1,0:T(8,128)(2,1)} async-done(((bf16[2048,1280]{1,0:T(8,128)(2,1)}), bf16[2048,1280]{1,0:T(8,128)(2,1)}) %all-reduce.2.cloned.1.call-update) | async-done | bytes 5242896 | tf_op jit(solution)/shard_map/psum | solution.py:15
  313.8 11.3 %fusion.2 = bf16[1280,1280]{1,0:T(8,128)(2,1)S(1)} fusion(bf16[2048,1280]{1,0:T(8,128)(2,1)} %all-reduce.2.cloned.1.call-done, bf16[2048,1280]{1,0:T(8,128)(2,1)} %bitcast, bf16[1280,1280]{1,0:T(8,128)(2,1)} %param.4), kind=kOutput, calls=%fused_computation.4 | convolution fusion | flops 6719078400 | bytes 17039360 | tf_op jit(solution)/shard_map/dot_general | solution.py:35
  325.1 1.7 copy-done.1
  326.8 0.7 slice.21
  327.5 0.0 reduce-scatter.2.cloned.1.call-start
  327.5 43.7 %all-gather.5.cloned.1.call-done = bf16[1024,1280]{1,0:T(8,128)(2,1)} async-done(((bf16[64,1280]{1,0:T(8,128)(2,1)}), bf16[1024,1280]{1,0:T(8,128)(2,1)}) %all-gather.5.cloned.1.call-update) | async-done | bytes 2621456 | tf_op jit(solution)/shard_map/all_gather | solution.py:44
  371.3 8.7 %convolution_bitcast_fusion = f32[1024,1280]{1,0:T(8,128)} fusion(bf16[1280,1280]{1,0:T(8,128)(2,1)} %copy-done.1, bf16[1024,1280]{1,0:T(8,128)(2,1)} %all-gather.5.cloned.1.call-done), kind=kOutput, calls=%fused_computation.6 | convolution fusion | flops 3355443200 | bytes 11141120 | tf_op jit(solution)/shard_map/dot_general | solution.py:19
  379.9 47.2 %all-gather.3.cloned.1.call-done = bf16[1024,1280]{1,0:T(8,128)(2,1)} async-done(((bf16[64,1280]{1,0:T(8,128)(2,1)}), bf16[1024,1280]{1,0:T(8,128)(2,1)}) %all-gather.3.cloned.1.call-update) | async-done | bytes 2621456 | tf_op jit(solution)/shard_map/all_gather | solution.py:43
  427.1 7.6 %fusion.21 = f32[1024,1280]{1,0:T(8,128)} fusion(bf16[1024,1280]{1,0:T(8,128)(2,1)} %all-gather.3.cloned.1.call-done, bf16[1280,1280]{1,0:T(8,128)(2,1)S(1)} %copy-done), kind=kOutput, calls=%fused_computation.37 | convolution fusion | flops 3355443200 | bytes 11141120 | tf_op jit(solution)/shard_map/dot_general | solution.py:19
  434.7 9.2 %pad_maximum_fusion = f32[1024,2560]{1,0:T(8,128)} fusion(f32[1024,1280]{1,0:T(8,128)} %convolution_bitcast_fusion, f32[1024,1280]{1,0:T(8,128)} %fusion.21), kind=kLoop, calls=%fused_computation | loop fusion | flops 2621440 | bytes 20971520 | tf_op jit(solution)/shard_map/concatenate | solution.py:63
  443.9 4.0 copy.6
  448.0 219.7 %reduce-scatter.2.cloned.1.call-done = f32[64,2560]{1,0:T(8,128)} async-done(((f32[1024,2560]{1,0:T(8,128)}), f32[64,2560]{1,0:T(8,128)}) %reduce-scatter.2.cloned.1.call-update) | async-done | bytes 655376 | tf_op jit(solution)/shard_map/reduce_scatter | solution.py:62
  667.7 2.3 fusion.17
  670.0 37.7 %psum.15 = f32[64]{0:T(128)S(1)} all-reduce(f32[64]{0:T(128)S(1)} %add_subtract_fusion), channel_id=1, replica_groups=mesh['row'=16,'col'=16] {'row'}, use_global_device_ids=true, to_apply=%region_5.6 | all-reduce | flops 64 | bytes 512 | tf_op jit(solution)/shard_map/psum | solution.py:74
  707.8 0.5 broadcast_multiply_fusion
  (9 shorter events, 0.1 us)
Async XLA Ops:
  11.0 128.4 %all-to-all-start = ((bf16[16,128,1280]{2,1,0:T(8,128)(2,1)}), bf16[16,128,1280]{2,1,0:T(8,128)(2,1)}, u32[]{:S(2)}, u32[]{:S(2)}) async-start(bf16[16,128,1280]{2,1,0:T(8,128)(2,1)} %stack.2), calls=%async_computation | async-start | bytes 10485760 | tf_op jit(solution)/shard_map/all_to_all | solution.py:32
  20.5 293.3 %all-reduce.2.cloned.1.call-start = ((), (), s32[]{:S(2)}) async-start(), calls=%async_computation.2 | async-start | bytes 10485760 | tf_op jit(solution)/shard_map/psum | solution.py:15
  144.6 1.9 copy-start
  144.6 226.7 %all-gather.5.cloned.1.call-start = ((), (), s32[]{:S(2)}) async-start(), calls=%async_computation.4 | async-start | bytes 2785280 | tf_op jit(solution)/shard_map/all_gather | solution.py:44
  147.2 279.9 %all-gather.3.cloned.1.call-start = ((), (), s32[]{:S(2)}) async-start(), calls=%async_computation.3 | async-start | bytes 2785280 | tf_op jit(solution)/shard_map/all_gather | solution.py:43
  325.1 1.7 copy-start.1
  327.5 340.2 %reduce-scatter.2.cloned.1.call-start = ((), (), s32[]{:S(2)}) async-start(), calls=%async_computation.5 | async-start | bytes 11141120 | tf_op jit(solution)/shard_map/reduce_scatter | solution.py:62
Sparse Core Ops, SparseCore 0:
  144.7 169.0 all-reduce.1
  317.1 54.0 all-gather.4
  374.0 53.0 all-gather.2
  444.0 223.6 reduce-scatter.1
